TPU v7x, 128 devices: a whole 4x4x4 slice. The times are simulated.
128 devices in a mesh: shard: 16 (over y, z), tensor: 4 (over x), section: 2 (over core).
Axes of the slice: x: 4, y: 4, z: 4, core: 2. Of those that a mesh axis runs over, the one named last changes fastest.
Arguments:
- attention_grads: float32 [16, 4, 768, 768], P('shard', 'section', 'tensor'), may hold values from -48 to 48
- feedforward_grads: float32 [16, 2, 3072, 768], P('shard', 'section', 'tensor'), may hold values from -48 to 48
- attention_errors: float32 [16, 4, 768, 768], P('shard', 'section', 'tensor'), may hold values from -3 to 3
- feedforward_errors: float32 [16, 2, 3072, 768], P('shard', 'section', 'tensor'), may hold values from -3 to 3
- attention_factor: float32 [4, 768, 32], P('section'), may hold values from -0.21875 to 0.21875
- feedforward_factor: float32 [2, 768, 32], P('section'), may hold values from -0.21875 to 0.21875
- attention_momentum: float32 [4, 768, 768], P('section', 'tensor', 'shard'), may hold values from -3 to 3
- feedforward_momentum: float32 [2, 3072, 768], P('section', 'tensor', 'shard'), may hold values from -3 to 3
- attention_master: float32 [4, 768, 768], P('section', 'tensor', 'shard'), may hold values from -3 to 3
- feedforward_master: float32 [2, 3072, 768], P('section', 'tensor', 'shard'), may hold values from -3 to 3
- gain_grads: float32 [16, 2, 768], P('shard', 'section', 'tensor'), may hold values from -6 to 6
- bias_grads: float32 [16, 12, 32], P('shard', 'tensor'), may hold values from -6 to 6
- gain_momentum: float32 [2, 768], P('section', 'tensor'), may hold values from -3 to 3
- gain_weight: float32 [2, 768], P('section', 'tensor'), may hold values from 0.5 to 1.5
- bias_momentum: float32 [12, 32], P('tensor'), may hold values from -3 to 3
- bias_weight: float32 [12, 32], P('tensor'), may hold values from -4 to 4
Outputs:
- attention_errors_new: float32 [16, 4, 768, 768], P('shard', 'section', 'tensor')
- feedforward_errors_new: float32 [16, 2, 3072, 768], P('shard', 'section', 'tensor')
- attention_factor_new: float32 [4, 768, 32], P('section')
- feedforward_factor_new: float32 [2, 768, 32], P('section')
- attention_momentum_new: float32 [4, 768, 768], P('section', 'tensor', 'shard')
- feedforward_momentum_new: float32 [2, 3072, 768], P('section', 'tensor', 'shard')
- attention_master_new: float32 [4, 768, 768], P('section', 'tensor', 'shard')
- feedforward_master_new: float32 [2, 3072, 768], P('section', 'tensor', 'shard')
- attention_fresh: bfloat16 [4, 768, 768], P('section', 'tensor')
- feedforward_fresh: bfloat16 [2, 3072, 768], P('section', 'tensor')
- gain_momentum_new: float32 [2, 768], P('section', 'tensor')
- gain_weight_new: float32 [2, 768], P('section', 'tensor')
- bias_momentum_new: float32 [12, 32], P('tensor')
- bias_weight_new: float32 [12, 32], P('tensor')
All inputs are finite; a program needn't handle non-finite values.
Results may differ from a plain program's by a relative error of at most 0.0004.
Values may be sent and summed in bfloat16 or wider, within the bound.
A program may use at most 64 MiB of HBM per device.

v0:
```python
import jax
import jax.numpy as jnp
from jax import lax
from jax.sharding import PartitionSpec as P

NS_STEPS = 5
exact_mode = lax.Precision.HIGHEST
learn_rate = 0.05
decay_rate = 0.9


def inverse_root(gram_matrix):
    identity = jnp.broadcast_to(
        jnp.eye(gram_matrix.shape[-1], dtype=jnp.float32), gram_matrix.shape
    )
    frob_scale = jnp.sqrt(jnp.sum(gram_matrix * gram_matrix, axis=(-2, -1), keepdims=True)) + 1e-06
    converge = gram_matrix / frob_scale
    inverse = identity
    for turn_index in range(NS_STEPS):
        middle = 0.5 * (3.0 * identity - jnp.matmul(inverse, converge, precision=exact_mode))
        converge, inverse = (
            jnp.matmul(converge, middle, precision=exact_mode),
            jnp.matmul(middle, inverse, precision=exact_mode),
        )
    return inverse / jnp.sqrt(frob_scale)


def left_terms(merged, factor):
    return jnp.einsum("rmij,mjk->mik", merged, factor, precision=exact_mode)


def row_gram(matrix):
    return jnp.einsum("mik,mil->mkl", matrix, matrix, precision=exact_mode)


def right_terms(merged, ortho):
    return jnp.einsum("rmij,mik->mjk", merged, ortho, precision=exact_mode)


def per_device(
    attention_grads,
    feedforward_grads,
    attention_errors,
    feedforward_errors,
    attention_factor,
    feedforward_factor,
    attention_momentum,
    feedforward_momentum,
    attention_master,
    feedforward_master,
    gain_grads,
    bias_grads,
    gain_momentum,
    gain_weight,
    bias_momentum,
    bias_weight,
):
    replicas = lax.axis_size("shard")
    column_width = attention_master.shape[2]
    column_start = lax.axis_index("shard") * column_width
    attention_base = attention_master - learn_rate * decay_rate * attention_momentum
    feedforward_base = feedforward_master - learn_rate * decay_rate * feedforward_momentum
    attention_merged = attention_grads + attention_errors
    feedforward_merged = feedforward_grads + feedforward_errors
    attention_part = left_terms(attention_merged, attention_factor)
    feedforward_part = left_terms(feedforward_merged, feedforward_factor)
    attention_power, feedforward_power = lax.psum((attention_part, feedforward_part), "shard")
    attention_gram, feedforward_gram = lax.psum(
        (row_gram(attention_power), row_gram(feedforward_power)), "tensor"
    )
    attention_ortho = jnp.matmul(
        attention_power, inverse_root(attention_gram), precision=exact_mode
    )
    feedforward_ortho = jnp.matmul(
        feedforward_power, inverse_root(feedforward_gram), precision=exact_mode
    )
    attention_back, feedforward_back = lax.psum(
        (
            right_terms(attention_merged, attention_ortho),
            right_terms(feedforward_merged, feedforward_ortho),
        ),
        ("shard", "tensor"),
    )
    attention_back = attention_back / replicas
    feedforward_back = feedforward_back / replicas
    attention_approx = jnp.einsum(
        "mik,mjk->mij", attention_ortho, attention_back, precision=exact_mode
    )
    feedforward_approx = jnp.einsum(
        "mik,mjk->mij", feedforward_ortho, feedforward_back, precision=exact_mode
    )
    attention_errors_new = attention_merged - attention_approx[None]
    feedforward_errors_new = feedforward_merged - feedforward_approx[None]
    attention_factor_new = jnp.matmul(
        attention_back, inverse_root(row_gram(attention_back)), precision=exact_mode
    )
    feedforward_factor_new = jnp.matmul(
        feedforward_back, inverse_root(row_gram(feedforward_back)), precision=exact_mode
    )
    attention_slice = lax.dynamic_slice_in_dim(attention_approx, column_start, column_width, 2)
    feedforward_slice = lax.dynamic_slice_in_dim(feedforward_approx, column_start, column_width, 2)
    attention_momentum_new = decay_rate * attention_momentum + attention_slice
    feedforward_momentum_new = decay_rate * feedforward_momentum + feedforward_slice
    attention_master_new = attention_base - learn_rate * attention_slice
    feedforward_master_new = feedforward_base - learn_rate * feedforward_slice
    attention_fresh, feedforward_fresh = (
        lax.all_gather(attention_master_new.astype(jnp.bfloat16), "shard", axis=2, tiled=True),
        lax.all_gather(feedforward_master_new.astype(jnp.bfloat16), "shard", axis=2, tiled=True),
    )
    gain_total, bias_total = lax.psum((gain_grads[0], bias_grads[0]), "shard")
    gain_momentum_new = decay_rate * gain_momentum + gain_total / replicas
    gain_weight_new = gain_weight - learn_rate * gain_momentum_new
    bias_momentum_new = decay_rate * bias_momentum + bias_total / replicas
    bias_weight_new = bias_weight - learn_rate * bias_momentum_new
    return (
        attention_errors_new,
        feedforward_errors_new,
        attention_factor_new,
        feedforward_factor_new,
        attention_momentum_new,
        feedforward_momentum_new,
        attention_master_new,
        feedforward_master_new,
        attention_fresh,
        feedforward_fresh,
        gain_momentum_new,
        gain_weight_new,
        bias_momentum_new,
        bias_weight_new,
    )


def solution(mesh):
    placed = (
        P("shard", "section", "tensor", None),
        P("shard", "section", "tensor", None),
        P("shard", "section", "tensor", None),
        P("shard", "section", "tensor", None),
        P("section", None, None),
        P("section", None, None),
        P("section", "tensor", "shard"),
        P("section", "tensor", "shard"),
        P("section", "tensor", "shard"),
        P("section", "tensor", "shard"),
        P("shard", "section", "tensor"),
        P("shard", "tensor", None),
        P("section", "tensor"),
        P("section", "tensor"),
        P("tensor", None),
        P("tensor", None),
    )
    return jax.shard_map(
        per_device,
        mesh=mesh,
        in_specs=placed,
        out_specs=(
            P("shard", "section", "tensor", None),
            P("shard", "section", "tensor", None),
            P("section", None, None),
            P("section", None, None),
            P("section", "tensor", "shard"),
            P("section", "tensor", "shard"),
            P("section", "tensor", "shard"),
            P("section", "tensor", "shard"),
            P("section", "tensor", None),
            P("section", "tensor", None),
            P("section", "tensor"),
            P("section", "tensor"),
            P("tensor", None),
            P("tensor", None),
        ),
        check_vma=False,
    )
```

profile of v0, /device:TPU:0, one launch (start us, length us, event | category | flops | bytes accessed | tf_op | source)
XLA Modules:
  0.0 321.8 jit_solution(5114528691584657770)
XLA Ops:
  7.3 3.2 copy.39
  10.5 2.0 copy.40
  12.4 2.7 add.70
  15.1 2.2 fusion.2
  17.4 1.8 add.68
  21.5 76.9 %all-reduce.1 = (f32[2,192,32]{1,2,0:T(8,128)S(1)}, f32[1,192]{1,0:T(1,128)S(1)}, f32[3,32]{1,0:T(4,128)S(1)}) all-reduce(f32[2,192,32]{1,2,0:T(8,128)S(1)} %fusion.6, f32[1,192]{1,0:T(1,128)S(1)} %bitcast.162, f32[3,32]{1,0:T(4,128)S(1)} %bitcast.161), channel_id=1, replica_groups=mesh['shard'=16,'tensor'=4,'section'=2] {'shard'}, use_global_device_ids=true, to_apply=%region_0.0 | all-reduce | flops 12576 | bytes 100608 | tf_op jit(solution)/shard_map/psum | solution.py:67
  98.6 3.7 %all-reduce.6.cloned.1.call-done = f32[768,32]{0,1:T(8,128)} async-done(((f32[768,32]{0,1:T(8,128)}), f32[768,32]{0,1:T(8,128)}) %all-reduce.6.cloned.1.call-update) | async-done | bytes 98320 | tf_op jit(solution)/shard_map/psum | solution.py:67
  103.6 17.4 %all-reduce.2 = (f32[2,32,32]{2,1,0:T(8,128)S(1)}, f32[1,32,32]{2,1,0:T(8,128)S(1)}) all-reduce(f32[2,32,32]{2,1,0:T(8,128)S(1)} %fusion.78, f32[1,32,32]{2,1,0:T(8,128)S(1)} %convolution_bitcast_fusion.1), channel_id=1, replica_groups=mesh['shard'=16,'tensor'=4,'section'=2] {'tensor'}, use_global_device_ids=true, to_apply=%region_1.0 | all-reduce | flops 3072 | bytes 24576 | tf_op jit(solution)/shard_map/psum | solution.py:68
  127.1 2.8 fusion.8
  130.5 1.4 fusion.4
  133.7 121.8 %all-reduce.8.cloned.1.call-done = (f32[2,768,32]{1,2,0:T(8,128)}, f32[1,768,32]{1,2,0:T(8,128)}) async-done(((f32[2,768,32]{1,2,0:T(8,128)}, f32[1,768,32]{1,2,0:T(8,128)}), (f32[2,768,32]{1,2,0:T(8,128)}, f32[1,768,32]{1,2,0:T(8,128)})) %all-reduce.8.cloned.1.call-update) | async-done | bytes 294928 | tf_op jit(solution)/shard_map/psum | solution.py:77
  255.5 1.8 multiply_reduce_fusion.2
  259.8 1.4 multiply_reduce_fusion
  264.2 4.5 %bitcast_subtract_fusion = (f32[1,1,768,768]{2,3,1,0:T(8,128)}, f32[768,768]{0,1:T(8,128)S(1)}) fusion(f32[1,1,768,768]{2,3,1,0:T(8,128)S(1)} %add.70, f32[768,32]{0,1:T(8,128)S(1)} %fusion.92, f32[1,768,32]{1,2,0:T(8,128)} %get-tuple-element.43), kind=kOutput, calls=%fused_computation | convolution fusion | flops 227106816 | bytes 7274496 | tf_op jit(solution)/shard_map/mik,mjk->mij/dot_general | solution.py:89
  268.7 2.6 bitcast_subtract_fusion.1
  272.1 1.9 fusion.77
  275.6 22.5 %all_gather.6 = bf16[2,192,768]{1,0,2:T(2,128)(2,1)S(1)} all-gather(bf16[2,192,48]{1,0,2:T(2,128)(2,1)} %copy.44), channel_id=1, replica_groups=mesh['shard'=16,'tensor'=4,'section'=2] {'shard'}, dimensions={2}, use_global_device_ids=true | all-gather | bytes 626688 | tf_op jit(solution)/shard_map/all_gather | solution.py:107
  298.2 2.0 copy.45
  300.1 1.7 copy.48
  301.8 1.7 copy.46
  303.5 1.7 copy.47
  305.2 1.8 convolution_bitcast_fusion
  311.0 1.9 all-gather.2.cloned.1.call-done
  312.9 2.4 copy.49
  (123 shorter events, 22.3 us)
Async XLA Ops:
  7.2 13.0 %copy-start = (f32[2,768,32]{1,2,0:T(8,128)S(1)}, f32[2,768,32]{1,2,0:T(8,128)}, u32[]{:S(2)}) copy-start(f32[2,768,32]{1,2,0:T(8,128)} %param.20) | copy-start | bytes 589828
  7.2 3.3 %copy-start.5 = (f32[1,1,768,768]{3,2,1,0:T(8,128)S(1)}, f32[1,1,768,768]{3,2,1,0:T(8,128)}, u32[]{:S(2)}) copy-start(f32[1,1,768,768]{3,2,1,0:T(8,128)} %param.19) | copy-start | bytes 7077892
  7.2 95.1 %all-reduce.6.cloned.1.call-start = ((), (), s32[]{:S(2)}) async-start(), calls=%async_computation | async-start | bytes 196608 | tf_op jit(solution)/shard_map/psum | solution.py:67
  12.4 2.7 copy-start.11
  15.1 2.3 copy-start.16
  17.3 238.1 %all-reduce.8.cloned.1.call-start = ((), (), s32[]{:S(2)}) async-start(), calls=%async_computation.2 | async-start | bytes 589824 | tf_op jit(solution)/shard_map/psum | solution.py:77
  17.4 4.0 %copy-start.17 = (f32[1,1,192]{2,1,0:T(1,128)S(1)}, f32[1,1,192]{2,1,0:T(1,128)}, u32[]{:S(2)}) copy-start(f32[1,1,192]{2,1,0:T(1,128)} %param.26) | copy-start | bytes 2308
  19.2 1.0 copy-start.1
  102.3 24.4 %copy-start.7 = (f32[768,32]{0,1:T(8,128)S(1)}, f32[768,32]{0,1:T(8,128)}, u32[]{:S(2)}) copy-start(f32[768,32]{0,1:T(8,128)} %all-reduce.6.cloned.1.call-done) | copy-start | bytes 294916
  124.1 6.4 %copy-start.2 = (f32[1,2,192,768]{3,2,1,0:T(8,128)S(1)}, f32[1,2,192,768]{3,2,1,0:T(8,128)}, u32[]{:S(2)}) copy-start(f32[1,2,192,768]{3,2,1,0:T(8,128)} %copy-done.1) | copy-start | bytes 3538948
  127.0 5.2 %copy-start.18 = (f32[1,192]{1,0:T(1,128)S(1)}, f32[1,192]{1,0:T(1,128)}, u32[]{:S(2)}) copy-start(f32[1,192]{1,0:T(1,128)} %param.29) | copy-start | bytes 2308
  127.0 5.2 %copy-start.19 = (f32[1,192]{1,0:T(1,128)S(1)}, f32[1,192]{1,0:T(1,128)}, u32[]{:S(2)}) copy-start(f32[1,192]{1,0:T(1,128)} %param.28) | copy-start | bytes 2308
  127.0 5.8 %copy-start.12 = (f32[2,192,48]{1,2,0:T(8,128)S(1)}, f32[2,192,48]{1,2,0:T(8,128)}, u32[]{:S(2)}) copy-start(f32[2,192,48]{1,2,0:T(8,128)} %param.22) | copy-start | bytes 221188
  127.0 5.9 %copy-start.13 = (f32[2,192,48]{1,2,0:T(8,128)S(1)}, f32[2,192,48]{1,2,0:T(8,128)}, u32[]{:S(2)}) copy-start(f32[2,192,48]{1,2,0:T(8,128)} %param.24) | copy-start | bytes 221188
  127.0 6.0 %copy-start.14 = (f32[3,32]{1,0:T(4,128)S(1)}, f32[3,32]{1,0:T(4,128)}, u32[]{:S(2)}) copy-start(f32[3,32]{1,0:T(4,128)} %param.31) | copy-start | bytes 1156
  127.1 6.0 %copy-start.15 = (f32[3,32]{1,0:T(4,128)S(1)}, f32[3,32]{1,0:T(4,128)}, u32[]{:S(2)}) copy-start(f32[3,32]{1,0:T(4,128)} %param.30) | copy-start | bytes 1156
  132.0 181.0 %all-gather.2.cloned.1.call-start = ((), (), s32[]{:S(2)}) async-start(), calls=%async_computation.1 | async-start | bytes 1253376 | tf_op jit(solution)/shard_map/all_gather | solution.py:108
  264.2 4.5 %copy-start.3 = (f32[1,2,192,768]{3,2,1,0:T(8,128)S(1)}, f32[1,2,192,768]{3,2,1,0:T(8,128)}, u32[]{:S(2)}) copy-start(f32[1,2,192,768]{3,2,1,0:T(8,128)} %copy-done.1) | copy-start | bytes 3538948
  264.2 4.5 %copy-start.6 = (f32[2,768,32]{1,2,0:T(8,128)S(1)}, f32[2,768,32]{1,2,0:T(8,128)}, u32[]{:S(2)}) copy-start(f32[2,768,32]{1,2,0:T(8,128)} %get-tuple-element.42) | copy-start | bytes 589828
  268.7 2.6 copy-start.9
  268.7 2.6 copy-start.10
  271.3 26.9 %copy-start.4 = (f32[1,1,768,768]{2,3,1,0:T(8,128)S(1)}, f32[1,1,768,768]{2,3,1,0:T(8,128)}, u32[]{:S(2)}) copy-start(f32[1,1,768,768]{2,3,1,0:T(8,128)} %get-tuple-element.65) | copy-start | bytes 7077892
  300.1 8.8 %copy-start.8 = (f32[2,32,32]{2,1,0:T(8,128)S(1)}, f32[2,32,32]{2,1,0:T(8,128)}, u32[]{:S(2)}) copy-start(f32[2,32,32]{2,1,0:T(8,128)} %fusion.93) | copy-start | bytes 24580
  300.1 9.6 %copy-start.20 = (f32[2]{0:T(128)S(1)}, f32[2]{0:T(128)}, u32[]{:S(2)}) copy-start(f32[2]{0:T(128)} %get-tuple-element.59) | copy-start | bytes 28
Sparse Core Ops, SparseCore 0:
  17.5 84.7 all-reduce.5
  132.1 123.3 all-reduce.7
  272.2 40.6 all-gather.1
where the time goes:
time: 322 us
  waiting for transfers between devices  128 us (40%)
  blocking collectives  117 us (36%)
  matrix products  35.2 us (11%)
  local copies, waits for them, and re-layouts  16.6 us (5%)
  between operations  15.8 us (5%)
  other arithmetic  9.61 us (3%)
    psum x1, waiting for transfers between devices, per_device(): lax.psum((right_terms(attention_merged, attention_ortho), right_terms(fee...  122 us
    psum x1, blocking collectives, per_device(): lax.psum((attention_part, feedforward_part), 'shard')  76.9 us
    all_gather x1, blocking collectives, per_device(): lax.all_gather(attention_master_new.astype(jnp.bfloat16), 'shard', axis=2...  22.5 us
    psum x1, blocking collectives, per_device(): lax.psum((row_gram(attention_power), row_gram(feedforward_power)), 'tensor')  17.4 us
    unnamed x52, local copies, waits for them, and re-layouts  15.9 us
  transfers between devices with their start and end apart: 3, of which 3 were waited for; matrix products, arithmetic and copies ran while one was open for 6% of the time, Pallas kernels for 0%

commit v1 on v0

--- a/solution.py
+++ b/solution.py
@@ -104,7 +104,15 @@
     attention_master_new = attention_base - learn_rate * attention_slice
     feedforward_master_new = feedforward_base - learn_rate * feedforward_slice
     attention_fresh, feedforward_fresh = (
-        lax.all_gather(attention_master_new.astype(jnp.bfloat16), "shard", axis=2, tiled=True),
+        jnp.concatenate(
+            lax.all_to_all(
+                jnp.stack([attention_master_new.astype(jnp.bfloat16)] * lax.axis_size("shard")),
+                "shard",
+                0,
+                0,
+            ),
+            axis=2,
+        ),
         lax.all_gather(feedforward_master_new.astype(jnp.bfloat16), "shard", axis=2, tiled=True),
     )
     gain_total, bias_total = lax.psum((gain_grads[0], bias_grads[0]), "shard")

time: 322 us -> 327 us (1.016)
  blocking collectives: 117 us -> 94.3 us
  waiting for transfers between devices: 128 us -> 145 us
  starting transfers between devices: 0.3 us -> 4.64 us
  matrix products: 35.2 us -> 39.2 us
    all_gather x1 -> x0, blocking collectives: 22.5 us -> none  [per_device(): lax.all_gather(attention_master_new.astype(jnp.bfloat16), 'shard', axis=2...]
    all_gather x1, waiting for transfers between devices: 1.95 us -> 20.2 us  [per_device(): lax.all_gather(feedforward_master_new.astype(jnp.bfloat16), 'shard', axis...]
    all_to_all x0 -> x1, starting transfers between devices: none -> 4.33 us  [per_device(): lax.all_to_all(jnp.stack([attention_master_new.astype(jnp.bfloat16)] * la...]
    unnamed x52 -> x46, local copies, waits for them, and re-layouts: 15.9 us -> 16.1 us
  transfers between devices with their start and end apart: 3 -> 4, of which waited for: 3 -> 3; matrix products, arithmetic and copies ran while one was open for 6% -> 7% of each run, Pallas kernels for 0% -> 0%
where the time goes in v1:
time: 327 us; the launch traced here: 326 us
  waiting for transfers between devices  145 us (44%)
  blocking collectives  94.3 us (29%)
  matrix products  39.2 us (12%)
  local copies, waits for them, and re-layouts  17.2 us (5%)
  between operations  15.8 us (5%)
  other arithmetic  9.65 us (3%)
  starting transfers between devices  4.64 us (1%)
    psum x1, waiting for transfers between devices, per_device(): lax.psum((right_terms(attention_merged, attention_ortho), right_terms(fee...  121 us
    psum x1, blocking collectives, per_device(): lax.psum((attention_part, feedforward_part), 'shard')  76.9 us
    all_gather x1, waiting for transfers between devices, per_device(): lax.all_gather(feedforward_master_new.astype(jnp.bfloat16), 'shard', axis...  20.2 us
    psum x1, blocking collectives, per_device(): lax.psum((row_gram(attention_power), row_gram(feedforward_power)), 'tensor')  17.4 us
    unnamed x46, local copies, waits for them, and re-layouts  16.1 us
    dot_general x20, matrix products, inverse_root(): jnp.matmul(middle, inverse, precision=exact_mode)  7.05 us
  transfers between devices with their start and end apart: 4, of which 3 were waited for; matrix products, arithmetic and copies ran while one was open for 7% of the time, Pallas kernels for 0%

profile of v1, /device:TPU:0, one launch (start us, length us, event | category | flops | bytes accessed | tf_op | source)
XLA Modules:
  0.0 325.7 jit_solution(17155772035560129326)
XLA Ops:
  7.3 3.2 copy.51
  10.5 2.0 copy.52
  12.4 2.7 add.70
  15.1 2.2 fusion.2
  17.4 1.8 add.68
  21.5 76.9 %all-reduce.1 = (f32[2,192,32]{1,2,0:T(8,128)S(1)}, f32[1,192]{1,0:T(1,128)S(1)}, f32[3,32]{1,0:T(4,128)S(1)}) all-reduce(f32[2,192,32]{1,2,0:T(8,128)S(1)} %fusion.6, f32[1,192]{1,0:T(1,128)S(1)} %bitcast.166, f32[3,32]{1,0:T(4,128)S(1)} %bitcast.165), channel_id=1, replica_groups=mesh['shard'=16,'tensor'=4,'section'=2] {'shard'}, use_global_device_ids=true, to_apply=%region_0.0 | all-reduce | flops 12576 | bytes 100608 | tf_op jit(solution)/shard_map/psum | solution.py:67
  98.6 3.7 %all-reduce.6.cloned.1.call-done = f32[768,32]{0,1:T(8,128)} async-done(((f32[768,32]{0,1:T(8,128)}), f32[768,32]{0,1:T(8,128)}) %all-reduce.6.cloned.1.call-update) | async-done | bytes 98320 | tf_op jit(solution)/shard_map/psum | solution.py:67
  103.6 17.4 %all-reduce.2 = (f32[2,32,32]{2,1,0:T(8,128)S(1)}, f32[1,32,32]{2,1,0:T(8,128)S(1)}) all-reduce(f32[2,32,32]{2,1,0:T(8,128)S(1)} %fusion.78, f32[1,32,32]{2,1,0:T(8,128)S(1)} %convolution_bitcast_fusion.1), channel_id=1, replica_groups=mesh['shard'=16,'tensor'=4,'section'=2] {'tensor'}, use_global_device_ids=true, to_apply=%region_1.0 | all-reduce | flops 3072 | bytes 24576 | tf_op jit(solution)/shard_map/psum | solution.py:68
  127.1 2.8 fusion.8
  130.5 1.4 fusion.4
  134.5 120.9 %all-reduce.8.cloned.1.call-done = (f32[2,768,32]{1,2,0:T(8,128)}, f32[1,768,32]{1,2,0:T(8,128)}) async-done(((f32[2,768,32]{1,2,0:T(8,128)}, f32[1,768,32]{1,2,0:T(8,128)}), (f32[2,768,32]{1,2,0:T(8,128)}, f32[1,768,32]{1,2,0:T(8,128)})) %all-reduce.8.cloned.1.call-update) | async-done | bytes 294928 | tf_op jit(solution)/shard_map/psum | solution.py:77
  255.5 1.8 multiply_reduce_fusion.2
  261.0 1.4 multiply_reduce_fusion
  265.4 4.5 %bitcast_subtract_fusion = (f32[1,1,768,768]{2,3,1,0:T(8,128)}, f32[768,768]{0,1:T(8,128)S(1)}) fusion(f32[1,1,768,768]{2,3,1,0:T(8,128)S(1)} %add.70, f32[768,32]{0,1:T(8,128)S(1)} %fusion.92, f32[1,768,32]{1,2,0:T(8,128)} %get-tuple-element.57), kind=kOutput, calls=%fused_computation | convolution fusion | flops 227106816 | bytes 7274496 | tf_op jit(solution)/shard_map/mik,mjk->mij/dot_general | solution.py:89
  270.0 2.6 bitcast_subtract_fusion.1
  273.3 1.9 fusion.77
  276.3 4.3 %all-to-all-start = ((bf16[16,2,192,48]{2,3,1,0:T(8,128)(2,1)}), bf16[16,2,192,48]{2,3,1,0:T(8,128)(2,1)S(1)}, u32[]{:S(2)}, u32[]{:S(2)}) async-start(bf16[16,2,192,48]{2,3,1,0:T(8,128)(2,1)} %stack.2), calls=%async_computation | async-start | bytes 1572864 | tf_op jit(solution)/shard_map/all_to_all | solution.py:108
  281.5 1.5 convolution_divide_fusion.2
  283.0 1.9 copy.59
  284.9 1.7 copy.60
  286.6 1.7 copy.61
  291.7 1.8 convolution_bitcast_fusion
  296.6 20.2 %all-gather.2.cloned.1.call-done = bf16[1,768,768]{1,2,0:T(8,128)(2,1)} async-done(((bf16[1,768,48]{1,2,0:T(8,128)(2,1)}), bf16[1,768,768]{1,2,0:T(8,128)(2,1)}) %all-gather.2.cloned.1.call-update) | async-done | bytes 1179664 | tf_op jit(solution)/shard_map/all_gather | solution.py:116
  316.8 2.4 copy.63
  (120 shorter events, 27.2 us)
Async XLA Ops:
  7.2 13.1 %copy-start = (f32[2,768,32]{1,2,0:T(8,128)S(1)}, f32[2,768,32]{1,2,0:T(8,128)}, u32[]{:S(2)}) copy-start(f32[2,768,32]{1,2,0:T(8,128)} %param.20) | copy-start | bytes 589828
  7.2 3.3 %copy-start.5 = (f32[1,1,768,768]{3,2,1,0:T(8,128)S(1)}, f32[1,1,768,768]{3,2,1,0:T(8,128)}, u32[]{:S(2)}) copy-start(f32[1,1,768,768]{3,2,1,0:T(8,128)} %param.19) | copy-start | bytes 7077892
  7.2 95.1 %all-reduce.6.cloned.1.call-start = ((), (), s32[]{:S(2)}) async-start(), calls=%async_computation.1 | async-start | bytes 196608 | tf_op jit(solution)/shard_map/psum | solution.py:67
  12.4 2.7 copy-start.10
  15.1 2.3 copy-start.14
  17.3 238.1 %all-reduce.8.cloned.1.call-start = ((), (), s32[]{:S(2)}) async-start(), calls=%async_computation.3 | async-start | bytes 589824 | tf_op jit(solution)/shard_map/psum | solution.py:77
  17.4 4.0 %copy-start.15 = (f32[1,1,192]{2,1,0:T(1,128)S(1)}, f32[1,1,192]{2,1,0:T(1,128)}, u32[]{:S(2)}) copy-start(f32[1,1,192]{2,1,0:T(1,128)} %param.26) | copy-start | bytes 2308
  19.2 1.0 copy-start.1
  102.3 24.4 %copy-start.7 = (f32[768,32]{0,1:T(8,128)S(1)}, f32[768,32]{0,1:T(8,128)}, u32[]{:S(2)}) copy-start(f32[768,32]{0,1:T(8,128)} %all-reduce.6.cloned.1.call-done) | copy-start | bytes 294916
  124.1 6.4 %copy-start.2 = (f32[1,2,192,768]{3,2,1,0:T(8,128)S(1)}, f32[1,2,192,768]{3,2,1,0:T(8,128)}, u32[]{:S(2)}) copy-start(f32[1,2,192,768]{3,2,1,0:T(8,128)} %copy-done.1) | copy-start | bytes 3538948
  127.0 5.2 %copy-start.16 = (f32[1,192]{1,0:T(1,128)S(1)}, f32[1,192]{1,0:T(1,128)}, u32[]{:S(2)}) copy-start(f32[1,192]{1,0:T(1,128)} %param.29) | copy-start | bytes 2308
  127.0 5.2 %copy-start.17 = (f32[1,192]{1,0:T(1,128)S(1)}, f32[1,192]{1,0:T(1,128)}, u32[]{:S(2)}) copy-start(f32[1,192]{1,0:T(1,128)} %param.28) | copy-start | bytes 2308
  127.0 5.8 %copy-start.11 = (f32[2,192,48]{1,2,0:T(8,128)S(1)}, f32[2,192,48]{1,2,0:T(8,128)}, u32[]{:S(2)}) copy-start(f32[2,192,48]{1,2,0:T(8,128)} %param.22) | copy-start | bytes 221188
  127.0 6.9 %copy-start.12 = (f32[3,32]{1,0:T(4,128)S(1)}, f32[3,32]{1,0:T(4,128)}, u32[]{:S(2)}) copy-start(f32[3,32]{1,0:T(4,128)} %param.31) | copy-start | bytes 1156
  127.0 6.9 %copy-start.13 = (f32[3,32]{1,0:T(4,128)S(1)}, f32[3,32]{1,0:T(4,128)}, u32[]{:S(2)}) copy-start(f32[3,32]{1,0:T(4,128)} %param.30) | copy-start | bytes 1156
  132.0 184.8 %all-gather.2.cloned.1.call-start = ((), (), s32[]{:S(2)}) async-start(), calls=%async_computation.2 | async-start | bytes 1253376 | tf_op jit(solution)/shard_map/all_gather | solution.py:116
  265.4 4.5 %copy-start.3 = (f32[1,2,192,768]{3,2,1,0:T(8,128)S(1)}, f32[1,2,192,768]{3,2,1,0:T(8,128)}, u32[]{:S(2)}) copy-start(f32[1,2,192,768]{3,2,1,0:T(8,128)} %copy-done.1) | copy-start | bytes 3538948
  265.4 4.5 %copy-start.6 = (f32[2,768,32]{1,2,0:T(8,128)S(1)}, f32[2,768,32]{1,2,0:T(8,128)}, u32[]{:S(2)}) copy-start(f32[2,768,32]{1,2,0:T(8,128)} %get-tuple-element.56) | copy-start | bytes 589828
  269.9 2.6 copy-start.8
  269.9 2.6 copy-start.9
  272.5 10.5 %copy-start.4 = (f32[1,1,768,768]{2,3,1,0:T(8,128)S(1)}, f32[1,1,768,768]{2,3,1,0:T(8,128)}, u32[]{:S(2)}) copy-start(f32[1,1,768,768]{2,3,1,0:T(8,128)} %get-tuple-element.79) | copy-start | bytes 7077892
  276.3 19.2 %all-to-all-start = ((bf16[16,2,192,48]{2,3,1,0:T(8,128)(2,1)}), bf16[16,2,192,48]{2,3,1,0:T(8,128)(2,1)S(1)}, u32[]{:S(2)}, u32[]{:S(2)}) async-start(bf16[16,2,192,48]{2,3,1,0:T(8,128)(2,1)} %stack.2), calls=%async_computation | async-start | bytes 1572864 | tf_op jit(solution)/shard_map/all_to_all | solution.py:108
Sparse Core Ops, SparseCore 0:
  17.5 84.7 all-reduce.5
  132.1 123.3 all-reduce.7
  273.4 43.3 all-gather.1
